TPU v7x, 256 devices: a whole 4x4x8 slice. The times are simulated.
256 devices in a mesh: dp: 16 (over x_lo, z), tensor: 16 (over x_hi, y, core).
Axes of the slice: x: 4 (x_hi: 2, x_lo: 2; x = x_hi * 2 + x_lo), y: 4, z: 8, core: 2. Of those that a mesh axis runs over, the one named last changes fastest.
Arguments:
- hidden: bfloat16 [4096, 8192], P('dp', 'tensor'), may hold values from -6 to 6
- connector: bfloat16 [8192, 3584], P('tensor'), may hold values from -0.0625 to 0.0625
- routing: int32 [4096, 1], P('dp'), may hold values from 0 to 15; in each aligned block of 256 rows (0 to 255, 256 to 511, ...) at most 32 rows name the same one
- talker_in: bfloat16 [8192, 3584], P(('dp', 'tensor')), may hold values from -6 to 6
- norm_gain: float32 [3584], replicated, may hold values from 0.25 to 1.75
- kv_weight: bfloat16 [3584, 1024], replicated, may hold values from -0.09375 to 0.09375
- kv_grad: bfloat16 [8192, 1024], P(('dp', 'tensor')), may hold values from -24 to 24
Outputs:
- hidden_grad: bfloat16 [4096, 8192], P('dp', 'tensor')
- connector_grad: float32 [8192, 3584], P('tensor', 'dp')
- kv_weight_grad: float32 [3584, 1024], P(None, ('dp', 'tensor'))
Inputs may be any that keep to these rules, and one draw needn't show every extreme that they name: `routing`: among the 256 rows of one index of dp, at most 32 go to one shard.
All inputs are finite; a program needn't handle non-finite values.
Results may differ from a plain program's by a relative error of at most 0.005.
Values may be sent and summed in bfloat16 or wider, within the bound.
A program may use at most 64 MiB of HBM per device.

v0:
```python
import math
import jax
import jax.numpy as jnp
from jax import lax
from jax.sharding import Mesh
from jax.sharding import PartitionSpec as P

TENSOR = ("tensor_0", "tensor_1", "tensor_2")
DP_TENSOR = ("dp", "tensor_0", "tensor_1", "tensor_2")
CONTRACT_LAST = (((1,), (1,)), ((), ()))
CONTRACT_FIRST = (((0,), (0,)), ((), ()))


def cut_along(value, dim, size):
    before, after = (value.shape[:dim], value.shape[dim + 1 :])
    return jnp.moveaxis(value.reshape(*before, size, -1, *after), dim, 0)


def sum_at_owner(value, axis, dim):
    size = lax.axis_size(axis)
    pieces = lax.all_to_all(cut_along(value, dim, size), axis, 0, 0, tiled=True)
    return jnp.sum(pieces, axis=0)


def sent_to_all(value, axis):
    copies = jnp.broadcast_to(value, (lax.axis_size(axis), *value.shape))
    return lax.all_to_all(copies, axis, split_axis=0, concat_axis=0, tiled=True)


def in_order(pieces, dim):
    dims = list(pieces.shape[1:])
    dims[dim] *= pieces.shape[0]
    return jnp.moveaxis(pieces, 0, dim).reshape(dims)


def gather_axes(value, axes, dim):
    far, near = axes
    pieces = sent_to_all(sent_to_all(value, far), near)
    return in_order(pieces.swapaxes(0, 1).reshape(-1, *value.shape), dim)


def on_device(hidden, connector, routing, talker_in, norm_gain, kv_weight, kv_grad):
    dp_count = lax.axis_size("dp")
    tensor_count = lax.axis_size(TENSOR)
    rows_dev = hidden.shape[0]
    capacity = talker_in.shape[0]
    factor = 1.0 / math.sqrt(rows_dev * dp_count)
    route_rows = routing[:, 0]
    shards = jnp.arange(tensor_count, dtype=jnp.int32)
    onehot = (route_rows[:, None] == shards[None, :]).astype(jnp.int32)
    ranks = jnp.sum((jnp.cumsum(onehot, axis=0) - 1) * onehot, axis=1)
    slot_ids = route_rows * capacity + ranks
    counts = jnp.sum(onehot, axis=0)
    tensor_pos = lax.axis_index(TENSOR)
    own_count = jnp.sum(jnp.where(shards == tensor_pos, counts, 0))
    usable = jnp.arange(capacity, dtype=jnp.int32) < own_count
    masked = jnp.where(usable[:, None], kv_grad, jnp.zeros_like(kv_grad))
    inputs = talker_in.astype(jnp.float32)
    inv_rms = lax.rsqrt(jnp.mean(inputs * inputs, axis=1, keepdims=True) + 1e-06)
    scaled = inputs * inv_rms
    normed = (scaled * norm_gain).astype(jnp.bfloat16)
    back_grad = lax.dot_general(
        masked, kv_weight, CONTRACT_LAST, preferred_element_type=jnp.float32
    )
    gain_back = norm_gain * back_grad
    talker_grad = (
        inv_rms * (gain_back - scaled * jnp.mean(gain_back * scaled, axis=1, keepdims=True))
    ).astype(jnp.bfloat16)
    col_count = masked.shape[1]
    per_dev = col_count // (dp_count * tensor_count)
    group_rows = lax.all_gather(normed, TENSOR, axis=0, tiled=True)
    regrouped = masked.reshape(capacity, dp_count, tensor_count, per_dev)
    regrouped = regrouped.transpose(0, 2, 1, 3).reshape(capacity, col_count)
    group_cols = lax.all_to_all(regrouped, TENSOR, split_axis=1, concat_axis=0, tiled=True)
    block_terms = (
        lax.dot_general(group_rows, group_cols, CONTRACT_FIRST, preferred_element_type=jnp.float32)
        * factor
    )
    kv_weight_grad = sum_at_owner(block_terms, "dp", 1)
    gathered = gather_axes(talker_grad, (("tensor_0", "tensor_1"), "tensor_2"), 0)
    row_grad = jnp.take(gathered, slot_ids, axis=0)
    hidden_grad = lax.dot_general(
        row_grad, connector, CONTRACT_LAST, preferred_element_type=jnp.float32
    ).astype(jnp.bfloat16)
    conn_terms = (
        lax.dot_general(hidden, row_grad, CONTRACT_FIRST, preferred_element_type=jnp.float32)
        * factor
    )
    connector_grad = lax.psum_scatter(conn_terms, "dp", scatter_dimension=1, tiled=True)
    return (hidden_grad, connector_grad, kv_weight_grad)


def solution(mesh):
    finer = Mesh(
        mesh.devices.reshape(mesh.shape["dp"], 2, 4, 2), ("dp", "tensor_0", "tensor_1", "tensor_2")
    )
    return jax.shard_map(
        on_device,
        mesh=finer,
        in_specs=(
            P("dp", TENSOR),
            P(TENSOR, None),
            P("dp", None),
            P(DP_TENSOR, None),
            P(),
            P(),
            P(DP_TENSOR, None),
        ),
        out_specs=(P("dp", TENSOR), P(TENSOR, "dp"), P(None, DP_TENSOR)),
        check_vma=False,
    )
```

profile of v0, /device:TPU:8, one launch (start us, length us, event | category | flops | bytes accessed | tf_op | source)
XLA Modules:
  0.0 196.0 jit_solution(6129102235819686993)
XLA Ops:
  8.0 0.0 copy-start
  8.0 0.0 all-gather.2.cloned.1.call-start
  8.1 1.1 fusion.8
  9.2 0.7 fusion.11
  9.9 0.6 reduce-window.6
  10.5 0.2 slice_reduce_fusion
  10.7 0.9 fusion.10
  11.6 0.6 fusion.12
  12.2 0.6 iota_compare_fusion.2
  12.9 1.0 copy.15
  13.9 0.0 copy-start.1
  13.9 0.0 copy-start.2
  13.9 5.6 %fusion.3 = (f32[32]{0:T(128)S(1)}, f32[32,3584]{1,0:T(8,128)S(1)}) fusion(bf16[32,3584]{1,0:T(8,128)(2,1)} %param.10, f32[32]{0:T(128)S(1)} %add_rsqrt_fusion, bf16[32,1024]{0,1:T(8,128)(2,1)S(1)} %broadcast_select_fusion.3, bf16[3584,1024]{1,0:T(8,128)(2,1)} %param.12, f32[3584]{0:T(1024)} %param.11), kind=kOutput, calls=%fused_computation.11 | convolution fusion | flops 235454432 | bytes 8108288 | tf_op jit(solution)/shard_map/dot_general | solution.py:62
  19.5 0.0 copy-start.3
  19.6 0.0 copy-done.1
  19.6 0.0 copy-done.2
  19.6 0.9 fusion.7
  20.4 0.0 all-gather.2.cloned.1.call-update
  20.5 1.4 broadcast_in_dim.41
  21.9 7.4 %all-to-all-start = ((bf16[8,32,3584]{2,1,0:T(8,128)(2,1)}), bf16[8,32,3584]{2,1,0:T(8,128)(2,1)S(1)}, u32[]{:S(2)}, u32[]{:S(2)}) async-start(bf16[8,32,3584]{2,1,0:T(8,128)(2,1)} %broadcast_in_dim.41), calls=%async_computation | async-start | bytes 3670016 | tf_op jit(solution)/shard_map/all_to_all | solution.py:27
  29.2 0.0 reduce-scatter.2.cloned.1.call-start
  29.2 0.0 copy-done.3
  29.3 25.4 %all-to-all-done = bf16[8,32,3584]{2,1,0:T(8,128)(2,1)S(1)} async-done(((bf16[8,32,3584]{2,1,0:T(8,128)(2,1)}), bf16[8,32,3584]{2,1,0:T(8,128)(2,1)S(1)}, u32[]{:S(2)}, u32[]{:S(2)}) %all-to-all-start) | async-done | bytes 1835040 | tf_op jit(solution)/shard_map/all_to_all | solution.py:27
  54.7 0.4 broadcast_in_dim.42
  55.1 6.7 %all_to_all.34 = bf16[2,8,32,3584]{3,2,1,0:T(8,128)(2,1)S(1)} all-to-all(bf16[2,8,32,3584]{3,2,1,0:T(8,128)(2,1)S(1)} %broadcast_in_dim.42), channel_id=1, replica_groups=mesh['dp'=16,'tensor_0'=2,'tensor_1'=4,'tensor_2'=2] {'tensor_2'}, dimensions={0} | all-to-all | bytes 7340032 | tf_op jit(solution)/shard_map/all_to_all | solution.py:27
  61.7 2.0 %copy.16 = bf16[8,2,32,3584]{3,2,1,0:T(8,128)(2,1)} copy(bf16[8,2,32,3584]{3,2,0,1:T(8,128)(2,1)S(1)} %bitcast.42) | data formatting | bytes 7340032 | tf_op jit(solution)/shard_map/transpose | solution.py:39
  63.8 6.0 %gather_fusion = bf16[256,3584]{1,0:T(8,128)(2,1)S(1)} fusion(bf16[512,3584]{1,0:T(8,128)(2,1)} %bitcast.41, s32[1024]{0:T(1024)S(1)} %pad_clamp_fusion), kind=kCustom, calls=%fused_computation | custom fusion | bytes 3671040 | tf_op jit(solution)/shard_map/jit(_take)/gather | solution.py:81
  69.8 0.0 copy-done
  69.8 4.2 %multiply_bitcast_fusion = f32[512,3584]{0,1:T(8,128)} fusion(bf16[256,512]{1,0:T(8,128)(2,1)S(1)} %copy-done, bf16[256,3584]{1,0:T(8,128)(2,1)S(1)} %gather_fusion, pred[256]{0:T(512)(128)(4,1)S(1)} %get-tuple-element.5), kind=kOutput, calls=%fused_computation.1 | convolution fusion | flops 942276608 | bytes 9437440 | tf_op jit(solution)/shard_map/dot_general | solution.py:86
  74.1 0.0 reduce-scatter.2.cloned.1.call-update
  74.1 0.3 copy.18
  74.4 0.1 reshape.71
  74.5 12.2 %all_to_all.35 = bf16[16,2,1024]{2,1,0:T(2,128)(2,1)S(1)} all-to-all(bf16[16,2,1024]{2,1,0:T(2,128)(2,1)S(1)} %reshape.71), channel_id=1, replica_groups=mesh['dp'=16,'tensor_0'=2,'tensor_1'=4,'tensor_2'=2] {'tensor_0','tensor..., dimensions={0} | all-to-all | bytes 131072 | tf_op jit(solution)/shard_map/all_to_all | solution.py:74
  86.7 0.1 reshape.72
  86.9 4.4 %all-gather.2.cloned.1.call-done = bf16[512,3584]{1,0:T(8,128)(2,1)} async-done(((bf16[32,3584]{1,0:T(8,128)(2,1)}), bf16[512,3584]{1,0:T(8,128)(2,1)}) %all-gather.2.cloned.1.call-update) | async-done | bytes 3670032 | tf_op jit(solution)/shard_map/all_gather | solution.py:71
  91.3 2.8 %convolution_multiply_fusion = f32[3584,64]{0,1:T(8,128)S(1)} fusion(bf16[512,3584]{1,0:T(8,128)(2,1)} %all-gather.2.cloned.1.call-done, bf16[512,64]{1,0:T(8,128)(2,1)S(1)} %bitcast.46), kind=kOutput, calls=%fused_computation.2 | convolution fusion | flops 235110400 | bytes 4653056 | tf_op jit(solution)/shard_map/dot_general | solution.py:76
  94.1 1.2 reshape.60
  95.3 7.2 %all-to-all-start.3 = ((f32[16,3584,4]{1,2,0:T(4,128)}), f32[16,3584,4]{1,2,0:T(4,128)S(1)}, u32[]{:S(2)}, u32[]{:S(2)}) async-start(f32[16,3584,4]{1,2,0:T(4,128)} %bitcast.43), calls=%async_computation.4 | async-start | bytes 1835008 | tf_op jit(solution)/shard_map/all_to_all | solution.py:21
  102.5 3.9 %convolution_convert_fusion = bf16[256,512]{1,0:T(8,128)(2,1)} fusion(bf16[512,3584]{1,0:T(8,128)(2,1)} %param.8, bf16[256,3584]{1,0:T(8,128)(2,1)S(1)} %gather_fusion, pred[256]{0:T(512)(128)(4,1)S(1)} %get-tuple-element.5), kind=kOutput, calls=%fused_computation.5 | convolution fusion | flops 940572672 | bytes 5767424 | tf_op jit(solution)/shard_map/dot_general | solution.py:82
  106.5 32.0 %all-to-all-done.3 = f32[16,3584,4]{1,2,0:T(4,128)S(1)} async-done(((f32[16,3584,4]{1,2,0:T(4,128)}), f32[16,3584,4]{1,2,0:T(4,128)S(1)}, u32[]{:S(2)}, u32[]{:S(2)}) %all-to-all-start.3) | async-done | bytes 917536 | tf_op jit(solution)/shard_map/all_to_all | solution.py:21
  138.4 0.8 reduce_sum.62
  139.2 49.3 %reduce-scatter.2.cloned.1.call-done = f32[512,224]{0,1:T(8,128)} async-done(((f32[512,3584]{0,1:T(8,128)}), f32[512,224]{0,1:T(8,128)}) %reduce-scatter.2.cloned.1.call-update) | async-done | bytes 458768 | tf_op jit(solution)/shard_map/reduce_scatter | solution.py:89
  (8 shorter events, 0.2 us)
Async XLA Ops:
  8.0 61.8 %copy-start = (bf16[256,512]{1,0:T(8,128)(2,1)S(1)}, bf16[256,512]{1,0:T(8,128)(2,1)}, u32[]{:S(2)}) copy-start(bf16[256,512]{1,0:T(8,128)(2,1)} %param.7) | copy-start | bytes 786436
  8.0 83.2 %all-gather.2.cloned.1.call-start = ((), (), s32[]{:S(2)}) async-start(), calls=%async_computation.6 | async-start | bytes 3899392 | tf_op jit(solution)/shard_map/all_gather | solution.py:71
  13.9 5.6 %copy-start.1 = (bf16[32,3584]{1,0:T(8,128)(2,1)S(1)}, bf16[32,3584]{1,0:T(8,128)(2,1)}, u32[]{:S(2)}) copy-start(bf16[32,3584]{1,0:T(8,128)(2,1)} %param.10) | copy-start | bytes 688132
  13.9 5.6 %copy-start.2 = (f32[3584]{0:T(1024)S(1)}, f32[3584]{0:T(1024)}, u32[]{:S(2)}) copy-start(f32[3584]{0:T(1024)} %param.11) | copy-start | bytes 43012
  19.5 9.7 %copy-start.3 = (s32[256,1]{0,1:T(1,128)S(1)}, s32[256,1]{0,1:T(1,128)}, u32[]{:S(2)}) copy-start(s32[256,1]{0,1:T(1,128)} %param.9) | copy-start | bytes 3076
  21.9 32.8 %all-to-all-start = ((bf16[8,32,3584]{2,1,0:T(8,128)(2,1)}), bf16[8,32,3584]{2,1,0:T(8,128)(2,1)S(1)}, u32[]{:S(2)}, u32[]{:S(2)}) async-start(bf16[8,32,3584]{2,1,0:T(8,128)(2,1)} %broadcast_in_dim.41), calls=%async_computation | async-start | bytes 3670016 | tf_op jit(solution)/shard_map/all_to_all | solution.py:27
  29.2 159.3 %reduce-scatter.2.cloned.1.call-start = ((), (), s32[]{:S(2)}) async-start(), calls=%async_computation.5 | async-start | bytes 7798784 | tf_op jit(solution)/shard_map/reduce_scatter | solution.py:89
  95.3 43.1 %all-to-all-start.3 = ((f32[16,3584,4]{1,2,0:T(4,128)}), f32[16,3584,4]{1,2,0:T(4,128)S(1)}, u32[]{:S(2)}, u32[]{:S(2)}) async-start(f32[16,3584,4]{1,2,0:T(4,128)} %bitcast.43), calls=%async_computation.4 | async-start | bytes 1835008 | tf_op jit(solution)/shard_map/all_to_all | solution.py:21
Sparse Core Ops, SparseCore 0:
  20.6 70.6 all-gather.1
Sparse Core Ops, SparseCore 1:
  74.2 114.3 reduce-scatter.1
where the time goes:
time: 196 us
  waiting for transfers between devices  111 us (57%)
  blocking collectives  18.9 us (10%)
  matrix products  16.6 us (8%)
  between operations  15.6 us (8%)
  starting transfers between devices  14.7 us (8%)
  local copies, waits for them, and re-layouts  12.8 us (7%)
  other arithmetic  6.28 us (3%)
    reduce_scatter x1, waiting for transfers between devices, on_device(): lax.psum_scatter(conn_terms, 'dp', scatter_dimension=1, tiled=True)  49.3 us
    all_to_all x1, waiting for transfers between devices, sum_at_owner(): pieces = lax.all_to_all(cut_along(value, dim, size), axis, 0, 0, tiled=True)  32 us
    all_to_all x1, waiting for transfers between devices, sent_to_all(): return lax.all_to_all(copies, axis, split_axis=0, concat_axis=0, tiled=True)  25.4 us
    all_to_all x1, blocking collectives, on_device(): lax.all_to_all(regrouped, TENSOR, split_axis=1, concat_axis=0, tiled=True)  12.2 us
    all_to_all x1, starting transfers between devices, sent_to_all(): return lax.all_to_all(copies, axis, split_axis=0, concat_axis=0, tiled=True)  7.38 us
    all_to_all x1, starting transfers between devices, sum_at_owner(): pieces = lax.all_to_all(cut_along(value, dim, size), axis, 0, 0, tiled=True)  7.24 us
    all_to_all x1, blocking collectives, sent_to_all(): return lax.all_to_all(copies, axis, split_axis=0, concat_axis=0, tiled=True)  6.68 us
    gather x1, local copies, waits for them, and re-layouts, on_device(): row_grad = jnp.take(gathered, slot_ids, axis=0)  6.04 us
  transfers between devices with their start and end apart: 4, of which 4 were waited for; matrix products, arithmetic and copies ran while one was open for 12% of the time, Pallas kernels for 0%

commit v1 on v0

--- a/solution.py
+++ b/solution.py
@@ -68,7 +68,8 @@
     ).astype(jnp.bfloat16)
     col_count = masked.shape[1]
     per_dev = col_count // (dp_count * tensor_count)
-    group_rows = lax.all_gather(normed, TENSOR, axis=0, tiled=True)
+    part_now = lax.all_to_all(jnp.stack([normed] * lax.axis_size(TENSOR)), TENSOR, 0, 0)
+    group_rows = jnp.concatenate(part_now, axis=0)
     regrouped = masked.reshape(capacity, dp_count, tensor_count, per_dev)
     regrouped = regrouped.transpose(0, 2, 1, 3).reshape(capacity, col_count)
     group_cols = lax.all_to_all(regrouped, TENSOR, split_axis=1, concat_axis=0, tiled=True)

time: 196 us -> 251 us (1.28); the launches traced: 196 us -> 247 us
  waiting for transfers between devices: 111 us -> 161 us
    all_to_all x0 -> x1, waiting for transfers between devices: none -> 117 us  [on_device(): lax.all_to_all(jnp.stack([normed] * lax.axis_size(TENSOR)), TENSOR, 0, 0)]
    reduce_scatter x1, waiting for transfers between devices: 49.3 us -> 0.01 us  [on_device(): lax.psum_scatter(conn_terms, 'dp', scatter_dimension=1, tiled=True)]
    all_to_all x1, waiting for transfers between devices: 32 us -> 21 us  [sum_at_owner(): pieces = lax.all_to_all(cut_along(value, dim, size), axis, 0, 0, tiled=True)]
    all_to_all x0 -> x1, starting transfers between devices: none -> 5.75 us  [on_device(): lax.all_to_all(jnp.stack([normed] * lax.axis_size(TENSOR)), TENSOR, 0, 0)]
    all_gather x1 -> x0, waiting for transfers between devices: 4.37 us -> none  [on_device(): group_rows = lax.all_gather(normed, TENSOR, axis=0, tiled=True)]
    all_to_all x1, starting transfers between devices: 7.24 us -> 3.63 us  [sum_at_owner(): pieces = lax.all_to_all(cut_along(value, dim, size), axis, 0, 0, tiled=True)]
  transfers between devices with their start and end apart: 4 -> 4, of which waited for: 4 -> 3; matrix products, arithmetic and copies ran while one was open for 12% -> 5% of each run, Pallas kernels for 0% -> 0%
where the time goes in v1:
time: 251 us; the launch traced here: 247 us
  waiting for transfers between devices  161 us (64%)
  blocking collectives  18.1 us (7%)
  starting transfers between devices  16.8 us (7%)
  matrix products  16.5 us (7%)
  local copies, waits for them, and re-layouts  15.1 us (6%)
  between operations  14.2 us (6%)
  other arithmetic  5.6 us (2%)
    all_to_all x1, waiting for transfers between devices, on_device(): lax.all_to_all(jnp.stack([normed] * lax.axis_size(TENSOR)), TENSOR, 0, 0)  117 us
    all_to_all x1, waiting for transfers between devices, sent_to_all(): return lax.all_to_all(copies, axis, split_axis=0, concat_axis=0, tiled=True)  23 us
    all_to_all x1, waiting for transfers between devices, sum_at_owner(): pieces = lax.all_to_all(cut_along(value, dim, size), axis, 0, 0, tiled=True)  21 us
    all_to_all x1, blocking collectives, on_device(): lax.all_to_all(regrouped, TENSOR, split_axis=1, concat_axis=0, tiled=True)  11.4 us
    all_to_all x1, starting transfers between devices, sent_to_all(): return lax.all_to_all(copies, axis, split_axis=0, concat_axis=0, tiled=True)  7.38 us
    all_to_all x1, blocking collectives, sent_to_all(): return lax.all_to_all(copies, axis, split_axis=0, concat_axis=0, tiled=True)  6.68 us
    gather x1, local copies, waits for them, and re-layouts, on_device(): row_grad = jnp.take(gathered, slot_ids, axis=0)  6.04 us
    all_to_all x1, starting transfers between devices, on_device(): lax.all_to_all(jnp.stack([normed] * lax.axis_size(TENSOR)), TENSOR, 0, 0)  5.75 us
  transfers between devices with their start and end apart: 4, of which 3 were waited for; matrix products, arithmetic and copies ran while one was open for 5% of the time, Pallas kernels for 0%

profile of v1, /device:TPU:8, one launch (start us, length us, event | category | flops | bytes accessed | tf_op | source)
XLA Modules:
  0.0 247.0 jit_solution(3805454367581694800)
XLA Ops:
  7.2 0.0 copy-start
  7.2 1.1 fusion.9
  8.3 0.7 fusion.13
  9.0 0.6 reduce-window.6
  9.6 0.2 slice_reduce_fusion
  9.8 0.9 fusion.12
  10.7 0.6 fusion.14
  11.3 0.6 iota_compare_fusion.2
  12.0 1.0 copy.16
  13.0 0.0 copy-start.1
  13.0 0.0 copy-start.2
  13.1 5.6 %fusion.4 = (f32[32]{0:T(128)S(1)}, f32[32,3584]{1,0:T(8,128)S(1)}) fusion(bf16[32,3584]{1,0:T(8,128)(2,1)} %param.10, f32[32]{0:T(128)S(1)} %add_rsqrt_fusion, bf16[32,1024]{0,1:T(8,128)(2,1)S(1)} %broadcast_select_fusion.3, bf16[3584,1024]{1,0:T(8,128)(2,1)} %param.12, f32[3584]{0:T(1024)} %param.11), kind=kOutput, calls=%fused_computation.12 | convolution fusion | flops 235454432 | bytes 8108288 | tf_op jit(solution)/shard_map/dot_general | solution.py:62
  18.7 0.0 copy-start.3
  18.7 0.0 copy-done.1
  18.7 0.0 copy-done.2
  18.7 0.2 fusion.8
  18.9 1.4 broadcast_in_dim.41
  20.3 7.4 %all-to-all-start = ((bf16[8,32,3584]{2,1,0:T(8,128)(2,1)}), bf16[8,32,3584]{2,1,0:T(8,128)(2,1)S(1)}, u32[]{:S(2)}, u32[]{:S(2)}) async-start(bf16[8,32,3584]{2,1,0:T(8,128)(2,1)} %broadcast_in_dim.41), calls=%async_computation | async-start | bytes 3670016 | tf_op jit(solution)/shard_map/all_to_all | solution.py:27
  27.7 0.0 reduce-scatter.2.cloned.1.call-start
  27.7 0.0 copy-done.3
  27.7 23.0 %all-to-all-done = bf16[8,32,3584]{2,1,0:T(8,128)(2,1)S(1)} async-done(((bf16[8,32,3584]{2,1,0:T(8,128)(2,1)}), bf16[8,32,3584]{2,1,0:T(8,128)(2,1)S(1)}, u32[]{:S(2)}, u32[]{:S(2)}) %all-to-all-start) | async-done | bytes 1835040 | tf_op jit(solution)/shard_map/all_to_all | solution.py:27
  50.7 0.4 broadcast_in_dim.42
  51.0 6.7 %all_to_all.36 = bf16[2,8,32,3584]{3,2,1,0:T(8,128)(2,1)S(1)} all-to-all(bf16[2,8,32,3584]{3,2,1,0:T(8,128)(2,1)S(1)} %broadcast_in_dim.42), channel_id=1, replica_groups=mesh['dp'=16,'tensor_0'=2,'tensor_1'=4,'tensor_2'=2] {'tensor_2'}, dimensions={0} | all-to-all | bytes 7340032 | tf_op jit(solution)/shard_map/all_to_all | solution.py:27
  57.7 2.0 copy.17
  59.7 6.0 %gather_fusion = bf16[256,3584]{1,0:T(8,128)(2,1)S(1)} fusion(bf16[512,3584]{1,0:T(8,128)(2,1)} %bitcast.48, s32[1024]{0:T(1024)S(1)} %pad_clamp_fusion), kind=kCustom, calls=%fused_computation | custom fusion | bytes 3671040 | tf_op jit(solution)/shard_map/jit(_take)/gather | solution.py:82
  65.8 0.0 copy-done
  65.8 4.2 %multiply_bitcast_fusion = f32[512,3584]{0,1:T(8,128)} fusion(bf16[256,512]{1,0:T(8,128)(2,1)S(1)} %copy-done, bf16[256,3584]{1,0:T(8,128)(2,1)S(1)} %gather_fusion, pred[256]{0:T(512)(128)(4,1)S(1)} %get-tuple-element.5), kind=kOutput, calls=%fused_computation.1 | convolution fusion | flops 942276608 | bytes 9437440 | tf_op jit(solution)/shard_map/dot_general | solution.py:87
  70.0 0.0 reduce-scatter.2.cloned.1.call-update
  70.1 0.3 copy.19
  70.4 0.1 reshape.75
  70.5 11.4 %all_to_all.37 = bf16[16,2,1024]{2,1,0:T(2,128)(2,1)S(1)} all-to-all(bf16[16,2,1024]{2,1,0:T(2,128)(2,1)S(1)} %reshape.75), channel_id=1, replica_groups=mesh['dp'=16,'tensor_0'=2,'tensor_1'=4,'tensor_2'=2] {'tensor_0','tensor..., dimensions={0} | all-to-all | bytes 131072 | tf_op jit(solution)/shard_map/all_to_all | solution.py:75
  81.9 2.3 stack.2
  84.2 5.8 %all-to-all-start.2 = ((bf16[16,32,3584]{2,1,0:T(8,128)(2,1)}), bf16[16,32,3584]{2,1,0:T(8,128)(2,1)}, u32[]{:S(2)}, u32[]{:S(2)}) async-start(bf16[16,32,3584]{2,1,0:T(8,128)(2,1)} %stack.2), calls=%async_computation.3 | async-start | bytes 7340032 | tf_op jit(solution)/shard_map/all_to_all | solution.py:71
  90.0 0.1 reshape.76
  90.1 116.8 %all-to-all-done.2 = bf16[16,32,3584]{2,1,0:T(8,128)(2,1)} async-done(((bf16[16,32,3584]{2,1,0:T(8,128)(2,1)}), bf16[16,32,3584]{2,1,0:T(8,128)(2,1)}, u32[]{:S(2)}, u32[]{:S(2)}) %all-to-all-start.2) | async-done | bytes 3670048 | tf_op jit(solution)/shard_map/all_to_all | solution.py:71
  206.9 2.8 %fusion = f32[3584,64]{0,1:T(8,128)S(1)} fusion(bf16[16,32,3584]{2,1,0:T(8,128)(2,1)} %all-to-all-done.2, bf16[16,32,64]{2,1,0:T(8,128)(2,1)S(1)} %reshape.76), kind=kOutput, calls=%fused_computation.3 | convolution fusion | flops 235110400 | bytes 4653056 | tf_op jit(solution)/shard_map/dot_general | solution.py:77
  209.7 1.2 reshape.63
  210.9 3.6 %all-to-all-start.4 = ((f32[16,3584,4]{1,2,0:T(4,128)}), f32[16,3584,4]{1,2,0:T(4,128)S(1)}, u32[]{:S(2)}, u32[]{:S(2)}) async-start(f32[16,3584,4]{1,2,0:T(4,128)} %bitcast.50), calls=%async_computation.5 | async-start | bytes 1835008 | tf_op jit(solution)/shard_map/all_to_all | solution.py:21
  214.6 3.9 %convolution_convert_fusion = bf16[256,512]{1,0:T(8,128)(2,1)} fusion(bf16[512,3584]{1,0:T(8,128)(2,1)} %param.8, bf16[256,3584]{1,0:T(8,128)(2,1)S(1)} %gather_fusion, pred[256]{0:T(512)(128)(4,1)S(1)} %get-tuple-element.5), kind=kOutput, calls=%fused_computation.6 | convolution fusion | flops 940572672 | bytes 5767424 | tf_op jit(solution)/shard_map/dot_general | solution.py:83
  218.4 21.0 %all-to-all-done.4 = f32[16,3584,4]{1,2,0:T(4,128)S(1)} async-done(((f32[16,3584,4]{1,2,0:T(4,128)}), f32[16,3584,4]{1,2,0:T(4,128)S(1)}, u32[]{:S(2)}, u32[]{:S(2)}) %all-to-all-start.4) | async-done | bytes 917536 | tf_op jit(solution)/shard_map/all_to_all | solution.py:21
  239.4 0.8 reduce_sum.62
  240.2 0.0 reduce-scatter.2.cloned.1.call-done
  (8 shorter events, 0.2 us)
Async XLA Ops:
  7.2 58.6 %copy-start = (bf16[256,512]{1,0:T(8,128)(2,1)S(1)}, bf16[256,512]{1,0:T(8,128)(2,1)}, u32[]{:S(2)}) copy-start(bf16[256,512]{1,0:T(8,128)(2,1)} %param.7) | copy-start | bytes 786436
  13.0 5.6 %copy-start.1 = (bf16[32,3584]{1,0:T(8,128)(2,1)S(1)}, bf16[32,3584]{1,0:T(8,128)(2,1)}, u32[]{:S(2)}) copy-start(bf16[32,3584]{1,0:T(8,128)(2,1)} %param.10) | copy-start | bytes 688132
  13.0 5.6 %copy-start.2 = (f32[3584]{0:T(1024)S(1)}, f32[3584]{0:T(1024)}, u32[]{:S(2)}) copy-start(f32[3584]{0:T(1024)} %param.11) | copy-start | bytes 43012
  18.7 9.0 %copy-start.3 = (s32[256,1]{0,1:T(1,128)S(1)}, s32[256,1]{0,1:T(1,128)}, u32[]{:S(2)}) copy-start(s32[256,1]{0,1:T(1,128)} %param.9) | copy-start | bytes 3076
  20.3 30.4 %all-to-all-start = ((bf16[8,32,3584]{2,1,0:T(8,128)(2,1)}), bf16[8,32,3584]{2,1,0:T(8,128)(2,1)S(1)}, u32[]{:S(2)}, u32[]{:S(2)}) async-start(bf16[8,32,3584]{2,1,0:T(8,128)(2,1)} %broadcast_in_dim.41), calls=%async_computation | async-start | bytes 3670016 | tf_op jit(solution)/shard_map/all_to_all | solution.py:27
  27.7 212.5 %reduce-scatter.2.cloned.1.call-start = ((), (), s32[]{:S(2)}) async-start(), calls=%async_computation.6 | async-start | bytes 7798784 | tf_op jit(solution)/shard_map/reduce_scatter | solution.py:90
  84.2 122.7 %all-to-all-start.2 = ((bf16[16,32,3584]{2,1,0:T(8,128)(2,1)}), bf16[16,32,3584]{2,1,0:T(8,128)(2,1)}, u32[]{:S(2)}, u32[]{:S(2)}) async-start(bf16[16,32,3584]{2,1,0:T(8,128)(2,1)} %stack.2), calls=%async_computation.3 | async-start | bytes 7340032 | tf_op jit(solution)/shard_map/all_to_all | solution.py:71
  210.9 28.5 %all-to-all-start.4 = ((f32[16,3584,4]{1,2,0:T(4,128)}), f32[16,3584,4]{1,2,0:T(4,128)S(1)}, u32[]{:S(2)}, u32[]{:S(2)}) async-start(f32[16,3584,4]{1,2,0:T(4,128)} %bitcast.50), calls=%async_computation.5 | async-start | bytes 1835008 | tf_op jit(solution)/shard_map/all_to_all | solution.py:21
Sparse Core Ops, SparseCore 0:
  70.2 93.5 reduce-scatter.1
